TPU v7x, 512 devices: a whole 4x8x8 slice. The times are simulated.
512 devices in a mesh: dp: 8 (over y), expert: 64 (over x, z, core).
Axes of the slice: x: 4, y: 8, z: 8, core: 2. Of those that a mesh axis runs over, the one named last changes fastest.
Arguments:
- tokens: bfloat16 [65536, 2048], P(('dp', 'expert')), may hold values from -6 to 6
- cotangent: bfloat16 [65536, 2048], P(('dp', 'expert')), may hold values from -6 to 6
- routes: int32 [65536, 2], P(('dp', 'expert')), may hold values from 0 to 63, all different within a row; in each aligned block of 128 rows (0 to 127, 128 to 255, ...) at most 6 rows name the same one
- gates: float32 [65536, 2], P(('dp', 'expert')), may hold values from 0.1 to 1
- w_gate: bfloat16 [64, 2048, 768], P('expert', None, 'dp'), may hold values from -0.125 to 0.125
- w_up: bfloat16 [64, 2048, 768], P('expert', None, 'dp'), may hold values from -0.125 to 0.125
- w_down: bfloat16 [64, 768, 2048], P('expert', 'dp'), may hold values from -0.21875 to 0.21875
Outputs:
- mixed: bfloat16 [65536, 2048], P(('dp', 'expert'))
- token_grad: bfloat16 [65536, 2048], P(('dp', 'expert'))
- gate_grad: float32 [65536, 2], P(('dp', 'expert'))
Inputs may be any that keep to these rules, and one draw needn't show every extreme that they name: `routes`: each row names 2 different experts. In each aligned block of 128 rows (the rows of one device), no expert is named by more than 6 rows, a bound that some block reaches.
All inputs are finite; a program needn't handle non-finite values.
Results may differ from a plain program's by a relative error of at most 0.014.
Values may be sent and summed in bfloat16 or wider, within the bound.
A program may use at most 64 MiB of HBM per device.

v0:
```python
import jax
import jax.numpy as jnp
from jax import lax
from jax.sharding import PartitionSpec as P


def forward_rows(rows, weight_rows, gate_w, up_w, down_w):
    pre_gate = jnp.dot(rows, gate_w, preferred_element_type=jnp.float32)
    pre_up = jnp.dot(rows, up_w, preferred_element_type=jnp.float32)
    sig = jax.nn.sigmoid(pre_gate)
    act = pre_gate * sig
    hidden = (act * pre_up).astype(jnp.bfloat16)
    raw_out = jnp.dot(hidden, down_w, preferred_element_type=jnp.float32)
    slot_out = (weight_rows[:, None] * raw_out).astype(jnp.bfloat16)
    return (slot_out, pre_gate, pre_up, hidden)


def backward_rows(back_rows, weight_rows, pre_gate, pre_up, hidden, gate_w, up_w, down_w):
    sig = jax.nn.sigmoid(pre_gate)
    act = pre_gate * sig
    back_hidden = jnp.dot(back_rows, down_w.T, preferred_element_type=jnp.float32)
    gate_part = jnp.sum(hidden.astype(jnp.float32) * back_hidden, axis=1)
    scaled = weight_rows[:, None] * back_hidden
    back_gate = (scaled * pre_up * sig * (1.0 + pre_gate * (1.0 - sig))).astype(jnp.bfloat16)
    back_up = (scaled * act).astype(jnp.bfloat16)
    slot_grad = jnp.dot(back_gate, gate_w.T, preferred_element_type=jnp.float32)
    slot_grad = (slot_grad + jnp.dot(back_up, up_w.T, preferred_element_type=jnp.float32)).astype(
        jnp.bfloat16
    )
    return (slot_grad, gate_part)


def body(tokens, cotangent, routes, gates, w_gate, w_up, w_down):
    tok_rows = tokens.shape[0]
    top_count = routes.shape[1]
    width = tokens.shape[1]
    experts = lax.axis_size("expert")
    capacity = max(2, 3 * tok_rows * top_count // (2 * experts))
    slots = tok_rows * top_count
    expert_ids = routes.reshape(slots)
    onehot = (expert_ids[:, None] == jnp.arange(experts, dtype=jnp.int32)[None, :]).astype(
        jnp.int32
    )
    slot_rank = jnp.sum(onehot * (jnp.cumsum(onehot, axis=0) - onehot), axis=1)
    slot_index = expert_ids * capacity + slot_rank
    table = (
        jnp.full((experts * capacity,), slots, jnp.int32)
        .at[slot_index]
        .set(jnp.arange(slots, dtype=jnp.int32))
    )
    live = table < slots
    source = jnp.where(live, table // top_count, 0)
    zero_rows = jnp.zeros((), jnp.bfloat16)
    x_slots = jnp.where(live[:, None], tokens[source], zero_rows).reshape(experts, capacity, width)
    dy_slots = jnp.where(live[:, None], cotangent[source], zero_rows).reshape(
        experts, capacity, width
    )
    gate_slots = jnp.where(live, gates.reshape(slots)[jnp.minimum(table, slots - 1)], 0.0).reshape(
        experts, capacity
    )
    gate_full, up_full, down_full = (
        lax.all_gather(w_gate, "dp", axis=2, tiled=True),
        lax.all_gather(w_up, "dp", axis=2, tiled=True),
        lax.all_gather(w_down, "dp", axis=1, tiled=True),
    )
    gate_w = gate_full[0]
    up_w = up_full[0]
    down_w = down_full[0]
    rows, weight_rows = (
        lax.all_to_all(x_slots, "expert", split_axis=0, concat_axis=0, tiled=True),
        lax.all_to_all(
            gate_slots.astype(jnp.bfloat16), "expert", split_axis=0, concat_axis=0, tiled=True
        ).astype(gate_slots.dtype),
    )
    flat_w = weight_rows.reshape(-1)
    slot_out, pre_gate, pre_up, hidden = forward_rows(
        rows.reshape(-1, width), flat_w, gate_w, up_w, down_w
    )
    out_back = lax.all_to_all(
        slot_out.reshape(experts, capacity, width),
        "expert",
        split_axis=0,
        concat_axis=0,
        tiled=True,
    )
    back_rows = lax.all_to_all(dy_slots, "expert", split_axis=0, concat_axis=0, tiled=True)
    slot_grad, gate_part = backward_rows(
        back_rows.reshape(-1, width), flat_w, pre_gate, pre_up, hidden, gate_w, up_w, down_w
    )
    grad_back, gate_back = (
        lax.all_to_all(
            slot_grad.reshape(experts, capacity, width),
            "expert",
            split_axis=0,
            concat_axis=0,
            tiled=True,
        ),
        lax.all_to_all(
            gate_part.reshape(experts, capacity).astype(jnp.bfloat16),
            "expert",
            split_axis=0,
            concat_axis=0,
            tiled=True,
        ).astype(jnp.float32),
    )
    out_rows = out_back.reshape(experts * capacity, width)[slot_index].reshape(
        tok_rows, top_count, width
    )
    mixed = jnp.sum(out_rows.astype(jnp.float32), axis=1).astype(jnp.bfloat16)
    grad_rows = grad_back.reshape(experts * capacity, width)[slot_index].reshape(
        tok_rows, top_count, width
    )
    token_grad = jnp.sum(grad_rows.astype(jnp.float32), axis=1).astype(jnp.bfloat16)
    gate_grad = gate_back.reshape(experts * capacity)[slot_index].reshape(tok_rows, top_count)
    return (mixed, token_grad, gate_grad)


def solution(mesh):
    return jax.shard_map(
        body,
        mesh=mesh,
        in_specs=(
            P(("dp", "expert"), None),
            P(("dp", "expert"), None),
            P(("dp", "expert"), None),
            P(("dp", "expert"), None),
            P("expert", None, "dp"),
            P("expert", None, "dp"),
            P("expert", "dp", None),
        ),
        out_specs=(P(("dp", "expert"), None), P(("dp", "expert"), None), P(("dp", "expert"), None)),
        check_vma=False,
    )
```

profile of v0, /device:TPU:1, one launch (start us, length us, event | category | flops | bytes accessed | tf_op | source)
XLA Modules:
  0.0 336.4 jit_solution(18263204052074881687)
XLA Ops:
  14.0 2.7 gather_fusion
  17.6 14.8 %all-to-all-start = ((bf16[64,1,6]{2,1,0:T(2,128)(2,1)}), bf16[64,1,6]{2,1,0:T(2,128)(2,1)S(1)}, u32[]{:S(2)}, u32[]{:S(2)}) async-start(bf16[64,1,6]{2,1,0:T(2,128)(2,1)} %convert_element_type.90), calls=%async_computation | async-start | bytes 65536 | tf_op jit(solution)/shard_map/all_to_all | solution.py:71
  32.6 3.1 gather_fusion.1
  35.7 2.5 gather.24
  38.2 3.1 gather_fusion.3
  41.3 3.8 %gather.27 = bf16[64,6,2048]{2,1,0:T(8,128)(2,1)} reshape(bf16[384,2048]{1,0:T(8,128)(2,1)} %gather_fusion.3) | data formatting | bytes 3145728 | tf_op jit(solution)/shard_map/gather | solution.py:55
  45.1 4.0 %broadcast_select_fusion.1 = (bf16[64,6,2048]{2,1,0:T(8,128)(2,1)}, bf16[64,6,2048]{2,1,0:T(8,128)(2,1)}) fusion(bf16[64,6,2048]{2,1,0:T(8,128)(2,1)S(1)} %gather.24, pred[64,6]{1,0:T(8,128)(4,1)S(1)} %broadcast_in_dim.40, bf16[64,6,2048]{2,1,0:T(8,128)(2,1)} %gather.27), kind=kLoop, calls=%fused_computation.22 | loop fusion | flops 1572864 | bytes 6291840 | tf_op jit(solution)/shard_map/jit(_where)/select_n | solution.py:54
  49.1 10.3 %all-to-all-start.1 = ((bf16[64,6,2048]{2,1,0:T(8,128)(2,1)}), bf16[64,6,2048]{2,1,0:T(8,128)(2,1)S(1)}, u32[]{:S(2)}, u32[]{:S(2)}) async-start(bf16[64,6,2048]{2,1,0:T(8,128)(2,1)} %get-tuple-element.13), calls=%async_computation.1 | async-start | bytes 4194304 | tf_op jit(solution)/shard_map/all_to_all | solution.py:70
  60.2 50.5 %all-to-all-done.1 = bf16[64,6,2048]{2,1,0:T(8,128)(2,1)S(1)} async-done(((bf16[64,6,2048]{2,1,0:T(8,128)(2,1)}), bf16[64,6,2048]{2,1,0:T(8,128)(2,1)S(1)}, u32[]{:S(2)}, u32[]{:S(2)}) %all-to-all-start.1) | async-done | bytes 1572896 | tf_op jit(solution)/shard_map/all_to_all | solution.py:70
  110.7 6.0 %all-to-all-start.3 = ((bf16[64,6,2048]{2,1,0:T(8,128)(2,1)}), bf16[64,6,2048]{2,1,0:T(8,128)(2,1)}, u32[]{:S(2)}, u32[]{:S(2)}) async-start(bf16[64,6,2048]{2,1,0:T(8,128)(2,1)} %get-tuple-element.14), calls=%async_computation.3 | async-start | bytes 4194304 | tf_op jit(solution)/shard_map/all_to_all | solution.py:86
  118.4 49.4 %all-to-all-done.3 = bf16[64,6,2048]{2,1,0:T(8,128)(2,1)} async-done(((bf16[64,6,2048]{2,1,0:T(8,128)(2,1)}), bf16[64,6,2048]{2,1,0:T(8,128)(2,1)}, u32[]{:S(2)}, u32[]{:S(2)}) %all-to-all-start.3) | async-done | bytes 1572896 | tf_op jit(solution)/shard_map/all_to_all | solution.py:86
  167.8 2.6 reshape.141
  170.5 4.8 %fusion.6 = f32[384,768]{1,0:T(8,128)} fusion(bf16[384,2048]{1,0:T(8,128)(2,1)} %reshape.137, bf16[1,2048,768]{1,2,0:T(8,128)(2,1)} %all-gather.6.cloned.1.call-done), kind=kOutput, calls=%fused_computation.13 | convolution fusion | flops 1207959552 | bytes 5898240 | tf_op jit(solution)/shard_map/dot_general | solution.py:9
  175.3 4.8 %fusion.10 = f32[384,768]{1,0:T(8,128)} fusion(bf16[384,2048]{1,0:T(8,128)(2,1)} %reshape.137, bf16[1,2048,768]{1,2,0:T(8,128)(2,1)} %all-gather.4.cloned.1.call-done), kind=kOutput, calls=%fused_computation.17 | convolution fusion | flops 1207959552 | bytes 5898240 | tf_op jit(solution)/shard_map/dot_general | solution.py:8
  180.1 5.3 %multiply_reduce_fusion = (bf16[384]{0:T(512)(128)(2,1)S(1)}, bf16[384,768]{1,0:T(8,128)(2,1)}, f32[384,768]{1,0:T(8,128)}) fusion(f32[384,768]{1,0:T(8,128)} %fusion.6, f32[384,768]{1,0:T(8,128)} %fusion.10, bf16[384,2048]{1,0:T(8,128)(2,1)S(1)} %reshape.141, bf16[1,768,2048]{2,1,0:T(8,128)(2,1)} %all-gather.8.cloned.1.call-done), kind=kOutput, calls=%fused_computation.23 | convolution fusion | flops 1210613376 | bytes 8848128 | tf_op jit(solution)/shard_map/dot_general | solution.py:21
  186.2 5.8 %all-to-all-start.5 = ((bf16[64,1,6]{2,1,0:T(2,128)(2,1)}), bf16[64,1,6]{2,1,0:T(2,128)(2,1)S(1)}, u32[]{:S(2)}, u32[]{:S(2)}) async-start(bf16[64,1,6]{2,1,0:T(2,128)(2,1)} %convert_element_type.91), calls=%async_computation.5 | async-start | bytes 65536 | tf_op jit(solution)/shard_map/all_to_all | solution.py:98
  192.0 3.5 %multiply_convert_fusion = bf16[384,2048]{1,0:T(8,128)(2,1)S(1)} fusion(bf16[384,768]{1,0:T(8,128)(2,1)} %get-tuple-element.10, bf16[1,768,2048]{2,1,0:T(8,128)(2,1)} %all-gather.8.cloned.1.call-done, f32[384]{0:T(512)S(1)} %reshape.146), kind=kOutput, calls=%fused_computation.20 | convolution fusion | flops 1209532416 | bytes 5309952 | tf_op jit(solution)/shard_map/dot_general | solution.py:13
  195.5 1.6 reshape.138
  197.1 4.1 %all-to-all-done.5 = bf16[64,1,6]{2,1,0:T(2,128)(2,1)S(1)} async-done(((bf16[64,1,6]{2,1,0:T(2,128)(2,1)}), bf16[64,1,6]{2,1,0:T(2,128)(2,1)S(1)}, u32[]{:S(2)}, u32[]{:S(2)}) %all-to-all-start.5) | async-done | bytes 800 | tf_op jit(solution)/shard_map/all_to_all | solution.py:98
  201.3 6.2 %all-to-all-start.2 = ((bf16[64,6,2048]{2,1,0:T(8,128)(2,1)}), bf16[64,6,2048]{2,1,0:T(8,128)(2,1)S(1)}, u32[]{:S(2)}, u32[]{:S(2)}) async-start(bf16[64,6,2048]{2,1,0:T(8,128)(2,1)} %reshape.138), calls=%async_computation.2 | async-start | bytes 4194304 | tf_op jit(solution)/shard_map/all_to_all | solution.py:79
  207.5 4.4 %fusion.4 = f32[384,2048]{1,0:T(8,128)S(1)} fusion(bf16[1,2048,768]{1,2,0:T(8,128)(2,1)} %all-gather.6.cloned.1.call-done, f32[384,768]{1,0:T(8,128)} %get-tuple-element.15, f32[384]{0:T(512)S(1)} %reshape.146, f32[384,768]{1,0:T(8,128)} %fusion.10), kind=kOutput, calls=%fused_computation.11 | convolution fusion | flops 1210023936 | bytes 8652288 | tf_op jit(solution)/shard_map/dot_general | solution.py:27
  212.0 2.8 add_convert_fusion
  214.9 3.7 %reshape.142 = bf16[64,6,2048]{2,1,0:T(8,128)(2,1)} reshape(bf16[384,2048]{1,0:T(8,128)(2,1)} %add_convert_fusion) | data formatting | bytes 3145728 | tf_op jit(solution)/shard_map/reshape | solution.py:92
  218.5 40.1 %all-to-all-done.2 = bf16[64,6,2048]{2,1,0:T(8,128)(2,1)S(1)} async-done(((bf16[64,6,2048]{2,1,0:T(8,128)(2,1)}), bf16[64,6,2048]{2,1,0:T(8,128)(2,1)S(1)}, u32[]{:S(2)}, u32[]{:S(2)}) %all-to-all-start.2) | async-done | bytes 1572896 | tf_op jit(solution)/shard_map/all_to_all | solution.py:79
  260.0 6.0 %all-to-all-start.4 = ((bf16[64,6,2048]{2,1,0:T(8,128)(2,1)}), bf16[64,6,2048]{2,1,0:T(8,128)(2,1)}, u32[]{:S(2)}, u32[]{:S(2)}) async-start(bf16[64,6,2048]{2,1,0:T(8,128)(2,1)} %reshape.142), calls=%async_computation.4 | async-start | bytes 4194304 | tf_op jit(solution)/shard_map/all_to_all | solution.py:91
  266.3 1.9 gather_fusion.5
  269.0 2.6 reshape.139
  273.0 1.5 reshape.140
  274.5 42.6 %all-to-all-done.4 = bf16[64,6,2048]{2,1,0:T(8,128)(2,1)} async-done(((bf16[64,6,2048]{2,1,0:T(8,128)(2,1)}), bf16[64,6,2048]{2,1,0:T(8,128)(2,1)}, u32[]{:S(2)}, u32[]{:S(2)}) %all-to-all-start.4) | async-done | bytes 1572896 | tf_op jit(solution)/shard_map/all_to_all | solution.py:91
  317.1 2.6 reshape.143
  322.6 3.6 %reduce_sum.46 = bf16[128,2048]{1,0:T(8,128)(2,1)} reduce(bf16[128,2,2048]{2,1,0:T(2,128)(2,1)S(1)} %copy-done.3, bf16[]{:T(256)} %constant.37.clone.1), dimensions={1}, to_apply=%region_4.5 | reduce | flops 262144 | bytes 1572866 | tf_op jit(solution)/shard_map/reduce_sum | solution.py:109
  326.3 3.6 %reduce_sum.47 = bf16[128,2048]{1,0:T(8,128)(2,1)} reduce(bf16[128,2,2048]{2,1,0:T(2,128)(2,1)S(1)} %copy-done.4, bf16[]{:T(256)} %constant.37.clone.1), dimensions={1}, to_apply=%region_5.6 | reduce | flops 262144 | bytes 1572866 | tf_op jit(solution)/shard_map/reduce_sum | solution.py:113
  (64 shorter events, 17.6 us)
Async XLA Ops:
  7.2 25.4 %copy-start = (bf16[128,2048]{1,0:T(8,128)(2,1)S(1)}, bf16[128,2048]{1,0:T(8,128)(2,1)}, u32[]{:S(2)}) copy-start(bf16[128,2048]{1,0:T(8,128)(2,1)} %param.7) | copy-start | bytes 1572868
  7.2 163.3 %all-gather.6.cloned.1.call-start = ((), (), s32[]{:S(2)}) async-start(), calls=%async_computation.7 | async-start | bytes 3538944 | tf_op jit(solution)/shard_map/all_gather | solution.py:63
  7.9 167.3 %all-gather.4.cloned.1.call-start = ((), (), s32[]{:S(2)}) async-start(), calls=%async_computation.6 | async-start | bytes 3538944 | tf_op jit(solution)/shard_map/all_gather | solution.py:62
  17.6 31.6 %all-to-all-start = ((bf16[64,1,6]{2,1,0:T(2,128)(2,1)}), bf16[64,1,6]{2,1,0:T(2,128)(2,1)S(1)}, u32[]{:S(2)}, u32[]{:S(2)}) async-start(bf16[64,1,6]{2,1,0:T(2,128)(2,1)} %convert_element_type.90), calls=%async_computation | async-start | bytes 65536 | tf_op jit(solution)/shard_map/all_to_all | solution.py:71
  35.7 2.6 copy-start.1
  49.1 61.5 %all-to-all-start.1 = ((bf16[64,6,2048]{2,1,0:T(8,128)(2,1)}), bf16[64,6,2048]{2,1,0:T(8,128)(2,1)S(1)}, u32[]{:S(2)}, u32[]{:S(2)}) async-start(bf16[64,6,2048]{2,1,0:T(8,128)(2,1)} %get-tuple-element.13), calls=%async_computation.1 | async-start | bytes 4194304 | tf_op jit(solution)/shard_map/all_to_all | solution.py:70
  59.5 120.6 %all-gather.8.cloned.1.call-start = ((), (), s32[]{:S(2)}) async-start(), calls=%async_computation.8 | async-start | bytes 3538944 | tf_op jit(solution)/shard_map/all_gather | solution.py:64
  110.7 57.1 %all-to-all-start.3 = ((bf16[64,6,2048]{2,1,0:T(8,128)(2,1)}), bf16[64,6,2048]{2,1,0:T(8,128)(2,1)}, u32[]{:S(2)}, u32[]{:S(2)}) async-start(bf16[64,6,2048]{2,1,0:T(8,128)(2,1)} %get-tuple-element.14), calls=%async_computation.3 | async-start | bytes 4194304 | tf_op jit(solution)/shard_map/all_to_all | solution.py:86
  186.2 15.1 %all-to-all-start.5 = ((bf16[64,1,6]{2,1,0:T(2,128)(2,1)}), bf16[64,1,6]{2,1,0:T(2,128)(2,1)S(1)}, u32[]{:S(2)}, u32[]{:S(2)}) async-start(bf16[64,1,6]{2,1,0:T(2,128)(2,1)} %convert_element_type.91), calls=%async_computation.5 | async-start | bytes 65536 | tf_op jit(solution)/shard_map/all_to_all | solution.py:98
  201.3 57.4 %all-to-all-start.2 = ((bf16[64,6,2048]{2,1,0:T(8,128)(2,1)}), bf16[64,6,2048]{2,1,0:T(8,128)(2,1)S(1)}, u32[]{:S(2)}, u32[]{:S(2)}) async-start(bf16[64,6,2048]{2,1,0:T(8,128)(2,1)} %reshape.138), calls=%async_computation.2 | async-start | bytes 4194304 | tf_op jit(solution)/shard_map/all_to_all | solution.py:79
  207.5 4.4 %copy-start.5 = (bf16[1,2048,768]{1,2,0:T(8,128)(2,1)S(1)}, bf16[1,2048,768]{1,2,0:T(8,128)(2,1)}, u32[]{:S(2)}) copy-start(bf16[1,2048,768]{1,2,0:T(8,128)(2,1)} %all-gather.4.cloned.1.call-done) | copy-start | bytes 9437188
  207.5 4.4 %copy-start.6 = (f32[384,768]{1,0:T(8,128)S(1)}, f32[384,768]{1,0:T(8,128)}, u32[]{:S(2)}) copy-start(f32[384,768]{1,0:T(8,128)} %fusion.10) | copy-start | bytes 3538948
  207.5 4.4 %copy-start.7 = (f32[384,768]{1,0:T(8,128)S(1)}, f32[384,768]{1,0:T(8,128)}, u32[]{:S(2)}) copy-start(f32[384,768]{1,0:T(8,128)} %get-tuple-element.15) | copy-start | bytes 3538948
  207.5 4.5 %copy-start.8 = (f32[384,768]{1,0:T(8,128)S(1)}, f32[384,768]{1,0:T(8,128)}, u32[]{:S(2)}) copy-start(f32[384,768]{1,0:T(8,128)} %fusion.6) | copy-start | bytes 3538948
  258.7 1.3 copy-start.2
  260.0 57.1 %all-to-all-start.4 = ((bf16[64,6,2048]{2,1,0:T(8,128)(2,1)}), bf16[64,6,2048]{2,1,0:T(8,128)(2,1)}, u32[]{:S(2)}, u32[]{:S(2)}) async-start(bf16[64,6,2048]{2,1,0:T(8,128)(2,1)} %reshape.142), calls=%async_computation.4 | async-start | bytes 4194304 | tf_op jit(solution)/shard_map/all_to_all | solution.py:91
  321.1 1.5 copy-start.3
  322.6 3.6 %copy-start.4 = (bf16[128,2,2048]{2,1,0:T(2,128)(2,1)S(1)}, bf16[128,2,2048]{2,1,0:T(2,128)(2,1)}, u32[]{:S(2)}) copy-start(bf16[128,2,2048]{2,1,0:T(2,128)(2,1)} %reshape.144) | copy-start | bytes 3145732
Sparse Core Ops, SparseCore 0:
  10.1 52.0 all-gather.5
  64.2 46.4 all-gather.3
  112.7 46.4 all-gather.7
where the time goes:
time: 337 us; the launch traced here: 336 us
  waiting for transfers between devices  189 us (56%)
  starting transfers between devices  49.3 us (15%)
  local copies, waits for them, and re-layouts  45.5 us (14%)
  matrix products  25.6 us (8%)
  between operations  14.1 us (4%)
  other arithmetic  13 us (4%)
    all_to_all x1, waiting for transfers between devices, body(): lax.all_to_all(x_slots, 'expert', split_axis=0, concat_axis=0, tiled=True)  50.5 us
    all_to_all x1, waiting for transfers between devices, body(): lax.all_to_all(dy_slots, 'expert', split_axis=0, concat_axis=0, tiled=True)  49.4 us
    all_to_all x1, waiting for transfers between devices, body(): lax.all_to_all(slot_grad.reshape(experts, capacity, width), 'expert', spl...  42.6 us
    all_to_all x1, waiting for transfers between devices, body(): lax.all_to_all(slot_out.reshape(experts, capacity, width), 'expert', spli...  40.1 us
    all_to_all x1, starting transfers between devices, body(): lax.all_to_all(gate_slots.astype(jnp.bfloat16), 'expert', split_axis=0, c...  14.8 us
    all_to_all x1, starting transfers between devices, body(): lax.all_to_all(x_slots, 'expert', split_axis=0, concat_axis=0, tiled=True)  10.3 us
    gather x2, local copies, waits for them, and re-layouts, body(): cotangent[source]  6.85 us
  transfers between devices with their start and end apart: 9, of which 5 were waited for; matrix products, arithmetic and copies ran while one was open for 19% of the time, Pallas kernels for 0%

commit v1 on v0

v1 whole, which is shorter than its diff:
```python
import functools

import jax
import jax.numpy as jnp
import numpy as np
from jax import lax
from jax.experimental import pallas as pl
from jax.experimental.pallas import tpu as pltpu
from jax.sharding import PartitionSpec as P

MESH = pl.DeviceIdType.MESH
CAP = 6
NC = 2
SIZES = {64: (4, 8)}
CHUNKS = 4
NT = (((1,), (1,)), ((), ()))


def log2(n):
    return n.bit_length() - 1


def kernel(
    nx, nz, ny,
    tok_ref, cot_ref, routes_ref, gates_ref, perm_ref, wg_ref, wu_ref, wd_ref,
    mixed_ref, grad_ref, gg_ref,
    pk, xr, zs, zr, w, pre_g, pre_u, hid, bg, bu, zo, zor, xo, xor, m0, m1,
    s_x, r_x, s_z, r_z, s_zo, r_zo, s_xo, r_xo, s_ring, r_ring, s_own, gate_sem,
):
    nk = nx * NC
    experts = nk * nz
    slots = experts * CAP
    tok, width = tok_ref.shape
    cw = width // CHUNKS
    fs = wg_ref.shape[0]
    half = fs // 2
    hops = ny // 2
    total = 2 * CHUNKS

    y = lax.axis_index("dp")
    e = lax.axis_index("expert")
    x, z, c = e // (nz * NC), (e // NC) % nz, e % NC

    def dev(dy, dx, dz, dc):
        return (
            lax.rem(y + dy + ny, ny),
            lax.rem(x + dx + nx, nx) * (nz * NC) + lax.rem(z + dz + nz, nz) * NC + lax.rem(c + dc, NC),
        )

    x_deltas = [(k // NC, k % NC) for k in range(nk)]
    to_x = [dev(0, dx, 0, dc) for dx, dc in x_deltas]
    from_x = [dev(0, -dx, 0, dc) for dx, dc in x_deltas]
    to_z = [dev(0, 0, dz, 0) for dz in range(nz)]
    from_z = [dev(0, 0, -dz, 0) for dz in range(nz)]
    ring_dev = (dev(1, 0, 0, 0), dev(-1, 0, 0, 0))
    partner = dev(0, 0, 0, 1)

    own = (hops - 1) * 2 * fs
    own_copies = [
        pltpu.make_async_copy(ref, w.at[i, pl.ds(own, fs), :], s_own.at[i])
        for i, ref in enumerate((wg_ref, wu_ref, wd_ref))
    ]
    for copy in own_copies:
        copy.start()

    barrier = pltpu.get_barrier_semaphore()
    peers = to_x[1:] + to_z[1:] + list(ring_dev)
    for d in peers:
        pl.semaphore_signal(barrier, inc=1, device_id=d, device_id_type=MESH)

    ids = [routes_ref[k : k + 1, :] for k in range(2)]
    expert_row = lax.broadcasted_iota(jnp.int32, (experts, tok), 0)
    hot = [(expert_row == i).astype(jnp.float32) for i in ids]
    earlier = (
        lax.broadcasted_iota(jnp.int32, (tok, tok), 0) < lax.broadcasted_iota(jnp.int32, (tok, tok), 1)
    ).astype(jnp.bfloat16)
    count = jnp.dot((hot[0] + hot[1]).astype(jnp.bfloat16), earlier, preferred_element_type=jnp.float32)
    slot_row = lax.broadcasted_iota(jnp.int32, (slots, tok), 0)
    hits = []
    for k in range(2):
        rank = jnp.sum(hot[k] * count, axis=0, keepdims=True).astype(jnp.int32)
        i = ids[k]
        dx = ((i >> log2(nz * NC)) - x) & (nx - 1)
        dz = (((i >> 1) & (nz - 1)) - z) & (nz - 1)
        dc = ((i & 1) - c) & 1
        slot = ((dx * NC + dc) * nz + dz) * CAP + rank
        hits.append((slot_row == slot).astype(jnp.float32))
    m0[...] = hits[0].T.astype(jnp.bfloat16)
    m1[...] = hits[1].T.astype(jnp.bfloat16)
    pack = (hits[0] + hits[1]).astype(jnp.bfloat16)

    pl.semaphore_wait(barrier, len(peers))

    def x_copy(n, k):
        return pltpu.make_async_remote_copy(
            src_ref=pk.at[n, k], dst_ref=xr.at[n, k], send_sem=s_x.at[n], recv_sem=r_x.at[n],
            device_id=to_x[k], device_id_type=MESH)

    def z_copy(n, dz):
        return pltpu.make_async_remote_copy(
            src_ref=zs.at[n, dz], dst_ref=zr.at[n, dz], send_sem=s_z.at[n], recv_sem=r_z.at[n],
            device_id=to_z[dz], device_id_type=MESH)

    def zo_copy(n, dz):
        return pltpu.make_async_remote_copy(
            src_ref=zo.at[n, dz], dst_ref=zor.at[n, dz], send_sem=s_zo.at[n], recv_sem=r_zo.at[n],
            device_id=from_z[dz], device_id_type=MESH)

    def xo_copy(n, k):
        return pltpu.make_async_remote_copy(
            src_ref=xo.at[n, k], dst_ref=xor.at[n, k], send_sem=s_xo.at[n], recv_sem=r_xo.at[n],
            device_id=from_x[k], device_id_type=MESH)

    def all_of(n, count_, src, dst, s_sem, r_sem):
        return pltpu.make_async_remote_copy(
            src_ref=src.at[n, pl.ds(1, count_ - 1)], dst_ref=dst.at[n, pl.ds(1, count_ - 1)],
            send_sem=s_sem.at[n], recv_sem=r_sem.at[n], device_id=partner, device_id_type=MESH)

    def x_all(n):
        return all_of(n, nk, pk, xr, s_x, r_x)

    def z_all(n):
        return all_of(n, nz, zs, zr, s_z, r_z)

    def zo_all(n):
        return all_of(n, nz, zo, zor, s_zo, r_zo)

    def xo_all(n):
        return all_of(n, nk, xo, xor, s_xo, r_xo)

    def dispatch(base, ref):
        def step(n, carry):
            cols = pl.ds(pl.multiple_of(n * cw, cw), cw)
            rows = jnp.dot(pack, ref[:, cols], preferred_element_type=jnp.float32).astype(jnp.bfloat16)
            rows = rows.reshape(nk, nz * CAP, cw)
            pk[base + n] = rows
            xr[base + n, 0] = rows[0]
            for k in range(1, nk):
                x_copy(base + n, k).start()
            return carry

        lax.fori_loop(0, CHUNKS, step, 0)

    pieces = 6

    def ring_row(direction, d, h):
        if isinstance(d, int) and d == 0:
            return own + h * half
        if isinstance(d, int) and d == hops:
            return own + fs + h * half
        return (d - 1) * 2 * fs + direction * fs + h * half

    def ring_copy(direction, d, i, h):
        src = pl.ds(ring_row(direction, d - 1, h), half)
        dst = pl.ds(ring_row(direction, d, h), half)
        at = i * 2 + h
        return pltpu.make_async_remote_copy(
            src_ref=w.at[i, src, :], dst_ref=w.at[i, dst, :],
            send_sem=s_ring.at[direction, d - 1, at], recv_sem=r_ring.at[direction, d - 1, at],
            device_id=ring_dev[direction], device_id_type=MESH)

    def goes(direction, d, h):
        return d < hops or h == direction

    def ring_start():
        for p in range(pieces):
            for direction in range(2):
                if goes(direction, 1, p % 2):
                    ring_copy(direction, 1, p // 2, p % 2).start()

    def ring_event(j):
        d, p = j // pieces + 1, j % pieces
        for direction in range(2):
            ring_copy(direction, d, p // 2, p % 2).wait_recv()
            if goes(direction, d + 1, p % 2):
                ring_copy(direction, d + 1, p // 2, p % 2).start()

    def ring_last():
        for i in range(3):
            for direction in range(2):
                ring_copy(direction, hops, i, direction).wait_recv()

    events = (hops - 1) * pieces

    def forward_chunk(n):
        x_all(n).wait_recv()
        rows = jnp.dot(perm_ref[...], xr[n].reshape(slots, cw), preferred_element_type=jnp.float32)
        rows = rows.astype(jnp.bfloat16).reshape(nz, nk * CAP, cw)
        zs[n] = rows
        zr[n, 0] = rows[0]
        for dz in range(1, nz):
            z_copy(n, dz).start()

    def wait_own():
        for copy in own_copies:
            copy.wait()

    wait_own()

    @pl.when(c == 0)
    def _():
        ring_start()

    dispatch(0, tok_ref)
    dispatch(CHUNKS, cot_ref)

    @pl.when(c == 0)
    def _():
        per = -(-events // total)
        for n in range(total):
            forward_chunk(n)
            for j in range(n * per, min(events, (n + 1) * per)):
                ring_event(j)
        ring_last()
        pl.semaphore_signal(gate_sem, inc=1, device_id=partner, device_id_type=MESH)

    @pl.when(c == 1)
    def _():
        def step(n, carry):
            forward_chunk(n)
            return carry

        lax.fori_loop(0, total, step, 0)
        pl.semaphore_wait(gate_sem, 1)
        ring_start()

    def wide(base):
        return jnp.concatenate([zr[base + n].reshape(slots, cw) for n in range(CHUNKS)], axis=1)

    for n in range(CHUNKS):
        z_all(n).wait_recv()
    for g in range(hops):
        @pl.when(c == 1)
        def _():
            if g < hops - 1:
                for j in range(g * pieces, (g + 1) * pieces):
                    ring_event(j)
            else:
                ring_last()

        span = pl.ds(g * 2 * fs, 2 * fs)
        rows = wide(0)
        gate = lax.dot_general(rows, w[0, span, :], NT, preferred_element_type=jnp.float32)
        up = lax.dot_general(rows, w[1, span, :], NT, preferred_element_type=jnp.float32)
        pre_g[g] = gate
        pre_u[g] = up
        hid[g] = (gate * jax.nn.sigmoid(gate) * up).astype(jnp.bfloat16)

    def ship(n, rows):
        rows = rows.astype(jnp.bfloat16).reshape(nz, nk * CAP, cw)
        zo[n] = rows
        zor[n, 0] = rows[0]
        for dz in range(1, nz):
            zo_copy(n, dz).start()

    def out_step(n, carry):
        cols = pl.ds(pl.multiple_of(n * cw, cw), cw)
        acc = jnp.zeros((slots, cw), jnp.float32)
        for g in range(hops):
            acc = acc + jnp.dot(
                hid[g], w[2, pl.ds(g * 2 * fs, 2 * fs), cols], preferred_element_type=jnp.float32)
        ship(n, acc)
        return carry

    lax.fori_loop(0, CHUNKS, out_step, 0)

    for n in range(CHUNKS):
        z_all(CHUNKS + n).wait_recv()

    def back_step(g, carry):
        span = pl.ds(pl.multiple_of(g * 2 * fs, 2 * fs), 2 * fs)
        back = lax.dot_general(wide(CHUNKS), w[2, span, :], NT, preferred_element_type=jnp.float32)
        gate, up = pre_g[g], pre_u[g]
        sig = jax.nn.sigmoid(gate)
        bg[g] = (back * up * sig * (1.0 + gate * (1.0 - sig))).astype(jnp.bfloat16)
        bu[g] = (back * (gate * sig)).astype(jnp.bfloat16)
        return carry

    lax.fori_loop(0, hops, back_step, 0)

    def grad_step(n, carry):
        cols = pl.ds(pl.multiple_of(n * cw, cw), cw)
        acc = jnp.zeros((slots, cw), jnp.float32)
        for g in range(hops):
            span = pl.ds(g * 2 * fs, 2 * fs)
            acc = acc + jnp.dot(bg[g], w[0, span, cols], preferred_element_type=jnp.float32)
            acc = acc + jnp.dot(bu[g], w[1, span, cols], preferred_element_type=jnp.float32)
        ship(CHUNKS + n, acc)
        return carry

    lax.fori_loop(0, CHUNKS, grad_step, 0)

    def back_chunk(n):
        zo_all(n).wait_recv()
        rows = jnp.dot(perm_ref[...], zor[n].reshape(slots, cw), preferred_element_type=jnp.float32)
        rows = rows.astype(jnp.bfloat16).reshape(nk, nz * CAP, cw)
        xo[n] = rows
        xor[n, 0] = rows[0]
        for k in range(1, nk):
            xo_copy(n, k).start()

    weight = [jnp.broadcast_to(gates_ref[k : k + 1, :], (tok, tok)).T[:, 0:1] for k in range(2)]

    def picked(n):
        xo_all(n).wait_recv()
        rows = xor[n].reshape(slots, cw)
        return (
            jnp.dot(m0[...], rows, preferred_element_type=jnp.float32),
            jnp.dot(m1[...], rows, preferred_element_type=jnp.float32),
        )

    def combine_out(n, sums):
        a, b = picked(n)
        cols = pl.ds(pl.multiple_of(n * cw, cw), cw)
        mixed_ref[:, cols] = (weight[0] * a + weight[1] * b).astype(jnp.bfloat16)
        cot = cot_ref[:, cols].astype(jnp.float32)
        return (
            sums[0] + jnp.sum(cot * a, axis=1, keepdims=True),
            sums[1] + jnp.sum(cot * b, axis=1, keepdims=True),
        )

    def combine_grad(n):
        a, b = picked(CHUNKS + n)
        cols = pl.ds(pl.multiple_of(n * cw, cw), cw)
        grad_ref[:, cols] = (weight[0] * a + weight[1] * b).astype(jnp.bfloat16)

    back_chunk(0)

    def out_loop(n, sums):
        back_chunk(n + 1)
        return combine_out(n, sums)

    sums = lax.fori_loop(
        0, CHUNKS, out_loop, (jnp.zeros((tok, 1), jnp.float32), jnp.zeros((tok, 1), jnp.float32)))
    for k in range(2):
        gg_ref[k : k + 1, :] = jnp.broadcast_to(sums[k], (tok, tok)).T[0:1, :]

    def grad_loop(n, carry):
        back_chunk(CHUNKS + n + 1)
        combine_grad(n)
        return carry

    lax.fori_loop(0, CHUNKS - 1, grad_loop, 0)
    combine_grad(CHUNKS - 1)

    def drain(n, carry):
        x_all(n).wait_send()
        z_all(n).wait_send()
        zo_all(n).wait_send()
        xo_all(n).wait_send()
        return carry

    lax.fori_loop(0, total, drain, 0)
    for d in range(1, hops + 1):
        for p in range(pieces):
            for direction in range(2):
                if goes(direction, d, p % 2):
                    ring_copy(direction, d, p // 2, p % 2).wait_send()


def body(tokens, cotangent, routes, gates, w_gate, w_up, w_down):
    tok, width = tokens.shape
    ny, ne = lax.axis_size("dp"), lax.axis_size("expert")
    nx, nz = SIZES[ne]
    nk = nx * NC
    fs = w_down.shape[1]
    slots = ne * CAP
    cw = width // CHUNKS
    total = 2 * CHUNKS
    hops = ny // 2
    assert nk == nz and fs % 2 == 0
    perm = np.zeros((slots, slots), np.float32)
    for a in range(nz):
        for b in range(nk):
            for r in range(CAP):
                perm[(a * nk + b) * CAP + r, (b * nz + a) * CAP + r] = 1.0
    vmem = pl.BlockSpec(memory_space=pltpu.VMEM)
    any_ = pl.BlockSpec(memory_space=pl.ANY)
    dma = pltpu.SemaphoreType.DMA
    blocks = pltpu.VMEM((total, nz, nk * CAP, cw), jnp.bfloat16)
    hidden = (hops, slots, 2 * fs)
    mixed, token_grad, gate_grad = pl.pallas_call(
        functools.partial(kernel, nx, nz, ny),
        out_shape=(
            jax.ShapeDtypeStruct((tok, width), jnp.bfloat16),
            jax.ShapeDtypeStruct((tok, width), jnp.bfloat16),
            jax.ShapeDtypeStruct((2, tok), jnp.float32),
        ),
        in_specs=[vmem, vmem, vmem, vmem, vmem, any_, any_, any_],
        out_specs=(vmem, vmem, vmem),
        scratch_shapes=[
            blocks, blocks, blocks, blocks,
            pltpu.VMEM((3, ny * fs, width), jnp.bfloat16),
            pltpu.VMEM(hidden, jnp.float32), pltpu.VMEM(hidden, jnp.float32),
            pltpu.VMEM(hidden, jnp.bfloat16), pltpu.VMEM(hidden, jnp.bfloat16), pltpu.VMEM(hidden, jnp.bfloat16),
            blocks, blocks, blocks, blocks,
            pltpu.VMEM((tok, slots), jnp.bfloat16), pltpu.VMEM((tok, slots), jnp.bfloat16),
            dma((total,)), dma((total,)), dma((total,)), dma((total,)),
            dma((total,)), dma((total,)), dma((total,)), dma((total,)),
            dma((2, hops, 6)), dma((2, hops, 6)), dma((3,)),
            pltpu.SemaphoreType.REGULAR,
        ],
        compiler_params=pltpu.CompilerParams(
            collective_id=0, has_side_effects=True, vmem_limit_bytes=63 * 1024 * 1024),
    )(
        tokens, cotangent, routes.T, gates.T, jnp.asarray(perm, jnp.bfloat16),
        jnp.swapaxes(w_gate, 1, 2)[0], jnp.swapaxes(w_up, 1, 2)[0], w_down[0],
    )
    return mixed, token_grad, gate_grad.T


def solution(mesh):
    return jax.shard_map(
        body,
        mesh=mesh,
        in_specs=(
            P(("dp", "expert"), None),
            P(("dp", "expert"), None),
            P(("dp", "expert"), None),
            P(("dp", "expert"), None),
            P("expert", None, "dp"),
            P("expert", None, "dp"),
            P("expert", "dp", None),
        ),
        out_specs=(P(("dp", "expert"), None), P(("dp", "expert"), None), P(("dp", "expert"), None)),
        check_vma=False,
    )
```

time: 337 us -> 172 us (0.51)
  waiting for transfers between devices: 189 us -> 0 us
  Pallas kernels: 0 us -> 168 us
  starting transfers between devices: 49.3 us -> 0 us
  local copies, waits for them, and re-layouts: 45.5 us -> 3.3 us
  matrix products: 25.6 us -> 0 us
  between operations: 14.1 us -> 0.65 us
  other arithmetic: 13 us -> 0 us
    all_to_all x6 -> x0, waiting for transfers between devices: 187 us -> none  [the longest x1 50.5 us: body(): lax.all_to_all(x_slots, 'expert', split_axis=0, concat_axis=0, tiled=True)]
    pallas_call x0 -> x1, Pallas kernels: none -> 168 us  [body(): pl.pallas_call(functools.partial(kernel, nx, nz, ny), out_shape=(jax.Shap...]
    all_to_all x6 -> x0, starting transfers between devices: 49.2 us -> none  [the longest x1 14.8 us: body(): lax.all_to_all(gate_slots.astype(jnp.bfloat16), 'expert', split_axis=0, c...]
    dot_general x6 -> x0, matrix products: 25.6 us -> none  [the longest x1 5.33 us: backward_rows(): jnp.dot(back_rows, down_w.T, preferred_element_type=jnp.float32)]
    gather x8 -> x0, local copies, waits for them, and re-layouts: 19.8 us -> none  [the longest x2 6.85 us: body(): cotangent[source]]
    reshape x10 -> x0, local copies, waits for them, and re-layouts: 17.8 us -> none  [the longest x2 4.12 us: body(): out_back.reshape(experts * capacity, width)[slot_index]]
    reduce_sum x3 -> x0, other arithmetic: 7.38 us -> none  [the longest x1 3.64 us: body(): mixed = jnp.sum(out_rows.astype(jnp.float32), axis=1).astype(jnp.bfloat16)]
    select_n x4 -> x0, other arithmetic: 4.07 us -> none  [the longest x1 4.05 us: body(): jnp.where(live[:, None], tokens[source], zero_rows)]
  transfers between devices with their start and end apart: 9 -> 0, of which waited for: 5 -> 0; matrix products, arithmetic and copies ran while one was open for 19% -> 0% of each run, Pallas kernels for 0% -> 0%
where the time goes in v1:
time: 172 us
  Pallas kernels  168 us (98%)
  local copies, waits for them, and re-layouts  3.3 us (2%)
    pallas_call x1, Pallas kernels, body(): pl.pallas_call(functools.partial(kernel, nx, nz, ny), out_shape=(jax.Shap...  168 us

profile of v1, /device:TPU:1, one launch (start us, length us, event | category | flops | bytes accessed | tf_op | source)
XLA Modules:
  0.0 172.1 jit_solution(11798285275193685233)
XLA Ops:
  0.6 168.2 %shard_map.103 = (bf16[128,2048]{1,0:T(8,128)(2,1)}, bf16[128,2048]{1,0:T(8,128)(2,1)}, f32[2,128]{1,0:T(2,128)}) custom-call(bf16[128,2048]{1,0:T(8,128)(2,1)} %tok_ref.1, bf16[128,2048]{1,0:T(8,128)(2,1)} %cot_ref.1, s32[2,128]{1,0:T(2,128)} %bitcast.13, f32[2,128]{1,0:T(2,128)} %bitcast.14, bf16[384,384]{1,0:T(8,128)(2,1)} %constant.2.clone.perm_ref, ...), custom_call_target="tpu_custom_call" | custom-call | tf_op jit(solution)/shard_map/pallas_call | solution.py:382
  168.8 0.0 copy-start
  168.8 1.9 %copy.14 = bf16[128,2048]{1,0:T(8,128)(2,1)} copy(bf16[128,2048]{1,0:T(8,128)(2,1)} %get-tuple-element.12) | data formatting | bytes 1048576
  170.8 0.0 copy-done
  170.8 0.0 copy-start.1
  170.8 0.8 copy.15
  171.5 0.0 copy-done.1
  171.6 0.6 copy.16
Async XLA Ops:
  168.8 2.0 %copy-start = (bf16[128,2048]{1,0:T(8,128)(2,1)S(1)}, bf16[128,2048]{1,0:T(8,128)(2,1)}, u32[]{:S(2)}) copy-start(bf16[128,2048]{1,0:T(8,128)(2,1)} %get-tuple-element.13) | copy-start | bytes 1572868
  170.8 0.8 copy-start.1
